TPU v7x, 32 devices: a whole 2x2x4 slice. The times are simulated.
32 devices in a mesh: lat: 4 (over z), lon: 8 (over y, x, core).
Axes of the slice: x: 2, y: 2, z: 4, core: 2. Of those that a mesh axis runs over, the one named last changes fastest.
Arguments:
- inputs: bfloat16 [128, 360, 512], P('lat', 'lon'), may hold values from -6 to 6
- metric: float32 [128, 360], P('lat', 'lon'), may hold values from 0.5 to 2
- kernel_one: float32 [9, 512], replicated, may hold values from -2 to 2
- kernel_two: float32 [9, 512], replicated, may hold values from -2 to 2
- widths: int32 [128], P('lat'), may hold values from 0 to 90, as said below
- zonal_gains: bfloat16 [128, 181], P('lat'), may hold values from -0.19921875 to 0.19921875
- norm_gain: float32 [512], replicated, may hold values from 0.5 to 1.5
- weight_in: bfloat16 [512, 1024], replicated, may hold values from -0.25 to 0.25
- weight_out: bfloat16 [1024, 512], replicated, may hold values from -0.1875 to 0.1875
Outputs:
- updated: bfloat16 [128, 360, 512], P('lat', 'lon')
Inputs may be any that keep to these rules, and one draw needn't show every extreme that they name: widths gives the zonal filter half-width of each latitude row.
All inputs are finite; a program needn't handle non-finite values.
Results may differ from a plain program's by a relative error of at most 0.0061.
Values may be sent and summed in bfloat16 or wider, within the bound.
A program may use at most 64 MiB of HBM per device.

v0:
```python
import jax
import jax.numpy as jnp
from jax import lax
from jax.sharding import PartitionSpec as P


def padded_2(cells, sides, width, closed):
    for axis, dim in sides:
        count = lax.axis_size(axis)
        ends = count if closed else count - 1
        head = lax.slice_in_dim(cells, 0, width, axis=dim)
        tail = lax.slice_in_dim(cells, cells.shape[dim] - width, cells.shape[dim], axis=dim)
        cells = jnp.concatenate(
            [
                lax.ppermute(tail, axis, [(i, (i + 1) % count) for i in range(ends)]),
                cells,
                lax.ppermute(head, axis, [((i + 1) % count, i) for i in range(ends)]),
            ],
            axis=dim,
        )
    return cells


def shifted(value, axis, steps):
    count = lax.axis_size(axis)
    pairs = [(source, (source + steps) % count) for source in range(count)]
    return lax.ppermute(value, axis, pairs)


def gelu_tanh(values):
    return jax.nn.gelu(values, approximate=True)


def stencil(extended, kernel):
    height = extended.shape[0] - 2
    breadth = extended.shape[1] - 2
    summed = jnp.zeros((height, breadth, extended.shape[2]), jnp.float32)
    for tap in range(9):
        row_shift = tap // 3
        col_shift = tap % 3
        piece = extended[row_shift : row_shift + height, col_shift : col_shift + breadth].astype(
            jnp.float32
        )
        summed = summed + kernel[tap] * piece
    return summed


def tap_matrix(gain_pad, row_width, tap_block, block_len, half_reach):
    first_tap = (tap_block * block_len).astype(jnp.int32)
    segment = lax.dynamic_slice_in_dim(gain_pad, first_tap, block_len, 0)
    tap_ids = first_tap + jnp.arange(block_len, dtype=jnp.int32)
    keep = jnp.abs(tap_ids - half_reach) <= row_width
    segment = jnp.where(keep, segment, jnp.zeros_like(segment))
    padded = jnp.concatenate([segment, jnp.zeros((block_len + 1,), segment.dtype)])
    return jnp.tile(padded, block_len)[: 2 * block_len * block_len].reshape(
        block_len, 2 * block_len
    )


def zonal_circle(circle, row_width, row_gains, first_block, block_count):
    circle_len = circle.shape[0]
    chans = circle.shape[1]
    block_len = circle_len // 8
    half_reach = circle_len // 4
    tap_blocks = 2 * half_reach // block_len + 1
    extended = jnp.concatenate(
        [circle[circle_len - half_reach :], circle, circle[: half_reach + block_len]], axis=0
    )
    blocked = extended.reshape(-1, block_len, chans)
    gain_pad = jnp.concatenate(
        [row_gains, jnp.zeros((tap_blocks * block_len - row_gains.shape[0],), row_gains.dtype)]
    )
    start_tap = jnp.zeros((), jnp.int32)
    stop_tap = jnp.full((), tap_blocks, jnp.int32)

    def add_block(tap_block, summed):
        matrix = tap_matrix(gain_pad, row_width, tap_block, block_len, half_reach)
        first_window = (first_block + tap_block).astype(jnp.int32)
        near = lax.dynamic_slice_in_dim(blocked, first_window, block_count, 0)
        after = lax.dynamic_slice_in_dim(blocked, first_window + 1, block_count, 0)
        window = jnp.concatenate([near, after], axis=1)
        return summed + jnp.einsum(
            "ab,pbc->pac", matrix, window, preferred_element_type=jnp.float32
        )

    return lax.fori_loop(
        start_tap, stop_tap, add_block, jnp.zeros((block_count, block_len, chans), jnp.float32)
    )


def filter_rows(circles, row_widths, row_gains, first_block, block_count):
    out_cols = block_count * (circles.shape[1] // 8)
    chans = circles.shape[2]

    def one_row(row, results):
        circle = lax.dynamic_index_in_dim(circles, row, 0, keepdims=False)
        row_width = lax.dynamic_index_in_dim(row_widths, row, 0, keepdims=False)
        row_gain = lax.dynamic_index_in_dim(row_gains, row, 0, keepdims=False)
        filtered = zonal_circle(circle, row_width, row_gain, first_block, block_count)
        filtered = filtered.reshape(out_cols, chans).astype(jnp.bfloat16)
        return lax.dynamic_update_index_in_dim(results, filtered, row, 0)

    empty = jnp.zeros((circles.shape[0], out_cols, chans), jnp.bfloat16)
    return lax.fori_loop(0, circles.shape[0], one_row, empty)


def local(
    inputs, metric, kernel_one, kernel_two, widths, zonal_gains, norm_gain, weight_in, weight_out
):
    lat_count = lax.axis_size("lat")
    lat_index = lax.axis_index("lat")
    lon_count = lax.axis_size("lon")
    lon_index = lax.axis_index("lon")
    rows_here = inputs.shape[0]
    channels = inputs.shape[2]

    def extend_local(field):
        sideways = padded_2(field, (("lon", 1),), 1, True)
        partner_top, partner_bottom = shifted((sideways[:1], sideways[-1:]), "lon", lon_count // 2)
        extended = padded_2(sideways, (("lat", 0),), 1, False)
        upper = jnp.where(lat_index == 0, partner_top, extended[:1])
        lower = jnp.where(lat_index == lat_count - 1, partner_bottom, extended[-1:])
        return jnp.concatenate([upper, extended[1:-1], lower], axis=0)

    weights_here = metric[:, :, None]
    first = (inputs.astype(jnp.float32) * weights_here).astype(jnp.bfloat16)
    stencil_one = stencil(extend_local(first), kernel_one)
    second = (weights_here * gelu_tanh(stencil_one)).astype(jnp.bfloat16)
    stencil_two = stencil(extend_local(second), kernel_two)
    mixed = (inputs.astype(jnp.float32) + stencil_two).astype(jnp.bfloat16)
    band_count = rows_here // lon_count
    band_start = lon_index * band_count
    band_widths = lax.dynamic_slice_in_dim(widths, band_start, band_count, 0)
    band_gains = lax.dynamic_slice_in_dim(zonal_gains, band_start, band_count, 0)
    filtered = filter_rows(
        lax.all_to_all(mixed, "lon", split_axis=0, concat_axis=1, tiled=True),
        band_widths,
        band_gains,
        0,
        8,
    )
    zonal = lax.all_to_all(filtered, "lon", split_axis=1, concat_axis=0, tiled=True)
    flat = mixed.reshape(-1, channels).astype(jnp.float32)
    scale = lax.rsqrt(jnp.mean(flat * flat, axis=1, keepdims=True) + 1e-06)
    normed = (flat * scale * norm_gain).astype(jnp.bfloat16)
    hidden = gelu_tanh(jnp.dot(normed, weight_in, preferred_element_type=jnp.float32)).astype(
        jnp.bfloat16
    )
    pointwise = jnp.dot(hidden, weight_out, preferred_element_type=jnp.float32)
    combined = flat + zonal.reshape(-1, channels).astype(jnp.float32) + pointwise
    return combined.astype(jnp.bfloat16).reshape(inputs.shape)


def solution(mesh):
    placed = (
        P("lat", "lon", None),
        P("lat", "lon"),
        P(),
        P(),
        P("lat"),
        P("lat", None),
        P(),
        P(),
        P(),
    )
    return jax.shard_map(
        local, mesh=mesh, in_specs=placed, out_specs=P("lat", "lon", None), check_vma=False
    )
```

profile of v0, /device:TPU:0, one launch (start us, length us, event | category | flops | bytes accessed | tf_op | source)
XLA Modules:
  0.0 168.4 jit_solution(2688615630618107918)
XLA Ops:
  0.0 2.4 %fusion.14 = bf16[32,45,512]{2,1,0:T(8,128)(2,1)S(1)} fusion(f32[32,45]{1,0:T(8,128)} %param.14, bf16[32,45,512]{2,0,1:T(8,128)(2,1)} %param.13), kind=kLoop, calls=%fused_computation.29 | loop fusion | flops 2211840 | bytes 2954880 | tf_op jit(solution)/shard_map/convert_element_type | solution.py:126
  3.0 2.9 %collective-permute-start.1 = (bf16[32,1,512]{2,1,0:T(2,128)(2,1)S(1)}, bf16[32,1,512]{2,1,0:T(2,128)(2,1)S(1)}, u32[]{:S(2)}, u32[]{:S(2)}) collective-permute-start(bf16[32,1,512]{2,1,0:T(2,128)(2,1)S(1)} %get-tuple-element.288), channel_id=1, source_target_pairs={{1,0},{2,1},{3,2},{4,3},{5,4},{6,5},{7,6},{0,7},{9,8},{10,9},{11,1... | collective-permute-start | bytes 98312 | tf_op jit(solution)/shard_map/ppermute | solution.py:17
  6.0 1.9 %collective-permute-done = bf16[32,1,512]{2,1,0:T(2,128)(2,1)S(1)} collective-permute-done((bf16[32,1,512]{2,1,0:T(2,128)(2,1)S(1)}, bf16[32,1,512]{2,1,0:T(2,128)(2,1)S(1)}, u32[]{:S(2)}, u32[]{:S(2)}) %collective-permute-start) | collective-permute-done | bytes 32800 | tf_op jit(solution)/shard_map/ppermute | solution.py:15
  7.9 2.3 %collective-permute-start.4 = (bf16[1,47,512]{2,1,0:T(8,128)(2,1)S(1)}, bf16[1,47,512]{2,1,0:T(8,128)(2,1)S(1)}, u32[]{:S(2)}, u32[]{:S(2)}) collective-permute-start(bf16[1,47,512]{2,1,0:T(8,128)(2,1)S(1)} %get-tuple-element.284), channel_id=1, source_target_pairs={{0,4},{1,5},{2,6},{3,7},{4,0},{5,1},{6,2},{7,3},{8,12},{9,13},{10,... | collective-permute-start | bytes 144392 | tf_op jit(solution)/shard_map/ppermute | solution.py:27
  11.7 4.6 %collective-permute-start.3 = (bf16[1,47,512]{2,1,0:T(8,128)(2,1)S(1)}, bf16[1,47,512]{2,1,0:T(8,128)(2,1)S(1)}, u32[]{:S(2)}, u32[]{:S(2)}) collective-permute-start(bf16[1,47,512]{2,1,0:T(8,128)(2,1)S(1)} %get-tuple-element.284), channel_id=1, source_target_pairs={{0,8},{8,16},{16,24},{1,9},{9,17},{17,25},{2,10},{10,18},{18,26},{... | collective-permute-start | bytes 144392 | tf_op jit(solution)/shard_map/ppermute | solution.py:15
  16.3 1.7 collective-permute-done.3
  18.0 2.0 %maximum_maximum_fusion = (bf16[33,47,512]{2,1,0:T(8,128)(2,1)S(1)}, bf16[33,47,512]{2,1,0:T(8,128)(2,1)S(1)}) fusion(bf16[32,1,512]{2,1,0:T(2,128)(2,1)S(1)} %collective-permute-done.1, bf16[32,45,512]{2,1,0:T(8,128)(2,1)S(1)} %fusion.14, bf16[32,1,512]{2,1,0:T(2,128)(2,1)S(1)} %collective-permute-done, bf16[1,47,512]{2,1,0:T(8,128)(2,1)S(1)} %broadcast_select_fusion.3, ...), kind=kLoop, calls=%fused_computation.44 | loop fusion | flops 12705792 | bytes 4812800 | tf_op jit(solution)/shard_map/concatenate | solution.py:123
  20.1 5.0 %fusion.24 = bf16[32,45,512]{2,1,0:T(8,128)(2,1)S(1)} fusion(bf16[32,45,512]{2,1,0:T(8,128)(2,1)S(1)} %fusion.14, bf16[33,47,512]{2,1,0:T(8,128)(2,1)S(1)} %get-tuple-element.282, bf16[32,1,512]{2,1,0:T(2,128)(2,1)S(1)} %collective-permute-done.1, bf16[32,1,512]{2,1,0:T(2,128)(2,1)S(1)} %collective-permute-done, ...), kind=kLoop, calls=%fused_computation.39 | loop fusion | flops 30965760 | bytes 11886208 | tf_op jit(solution)/shard_map/convert_element_type | solution.py:128
  25.2 2.6 %collective-permute-start.7 = (bf16[32,1,512]{2,1,0:T(2,128)(2,1)S(1)}, bf16[32,1,512]{2,1,0:T(2,128)(2,1)S(1)}, u32[]{:S(2)}, u32[]{:S(2)}) collective-permute-start(bf16[32,1,512]{2,1,0:T(2,128)(2,1)S(1)} %get-tuple-element.286), channel_id=1, source_target_pairs={{1,0},{2,1},{3,2},{4,3},{5,4},{6,5},{7,6},{0,7},{9,8},{10,9},{11,1... | collective-permute-start | bytes 98312 | tf_op jit(solution)/shard_map/ppermute | solution.py:17
  27.9 1.9 %collective-permute-done.6 = bf16[32,1,512]{2,1,0:T(2,128)(2,1)S(1)} collective-permute-done((bf16[32,1,512]{2,1,0:T(2,128)(2,1)S(1)}, bf16[32,1,512]{2,1,0:T(2,128)(2,1)S(1)}, u32[]{:S(2)}, u32[]{:S(2)}) %collective-permute-start.6) | collective-permute-done | bytes 32800 | tf_op jit(solution)/shard_map/ppermute | solution.py:15
  29.9 2.7 %collective-permute-start.10 = (bf16[1,47,512]{2,1,0:T(8,128)(2,1)S(1)}, bf16[1,47,512]{2,1,0:T(8,128)(2,1)S(1)}, u32[]{:S(2)}, u32[]{:S(2)}) collective-permute-start(bf16[1,47,512]{2,1,0:T(8,128)(2,1)S(1)} %get-tuple-element.280), channel_id=1, source_target_pairs={{0,4},{1,5},{2,6},{3,7},{4,0},{5,1},{6,2},{7,3},{8,12},{9,13},{10,... | collective-permute-start | bytes 144392 | tf_op jit(solution)/shard_map/ppermute | solution.py:27
  34.1 4.9 %collective-permute-start.9 = (bf16[1,47,512]{2,1,0:T(8,128)(2,1)S(1)}, bf16[1,47,512]{2,1,0:T(8,128)(2,1)S(1)}, u32[]{:S(2)}, u32[]{:S(2)}) collective-permute-start(bf16[1,47,512]{2,1,0:T(8,128)(2,1)S(1)} %get-tuple-element.280), channel_id=1, source_target_pairs={{0,8},{8,16},{16,24},{1,9},{9,17},{17,25},{2,10},{10,18},{18,26},{... | collective-permute-start | bytes 144392 | tf_op jit(solution)/shard_map/ppermute | solution.py:15
  39.0 1.7 collective-permute-done.9
  40.7 2.0 %maximum_maximum_fusion.1 = (bf16[33,47,512]{2,1,0:T(8,128)(2,1)S(1)}, bf16[33,47,512]{2,1,0:T(8,128)(2,1)S(1)}) fusion(bf16[32,1,512]{2,1,0:T(2,128)(2,1)S(1)} %collective-permute-done.7, bf16[32,45,512]{2,1,0:T(8,128)(2,1)S(1)} %fusion.24, bf16[32,1,512]{2,1,0:T(2,128)(2,1)S(1)} %collective-permute-done.6, ...), kind=kLoop, calls=%fused_computation.46 | loop fusion | flops 12705792 | bytes 4812800 | tf_op jit(solution)/shard_map/concatenate | solution.py:123
  42.8 6.7 %multiply_reduce_fusion = (f32[32,45]{1,0:T(8,128)S(1)}, bf16[32,45,512]{2,1,0:T(8,128)(2,1)}) fusion(bf16[33,47,512]{2,1,0:T(8,128)(2,1)S(1)} %get-tuple-element.278, f32[512]{0:T(512)S(1)} %bitcast.75, f32[512]{0:T(512)S(1)} %bitcast.76, f32[512]{0:T(512)S(1)} %bitcast.69, bf16[32,1,512]{2,1,0:T(2,128)(2,1)S(1)} %collective-permute-done.7, ...), kind=kLoop, calls=%fused_computation.40 | loop fusion | flops 28015200 | bytes 13360768 | tf_op jit(solution)/shard_map/reduce_sum | solution.py:144
  49.5 3.7 %all-to-all-start = ((bf16[32,45,512]{2,1,0:T(8,128)(2,1)}), bf16[32,45,512]{2,1,0:T(8,128)(2,1)S(1)}, u32[]{:S(2)}, u32[]{:S(2)}) async-start(bf16[32,45,512]{2,1,0:T(8,128)(2,1)} %get-tuple-element.274), calls=%async_computation | async-start | bytes 3145728 | tf_op jit(solution)/shard_map/all_to_all | solution.py:136
  54.0 20.1 %all-to-all-done = bf16[32,45,512]{2,1,0:T(8,128)(2,1)S(1)} async-done(((bf16[32,45,512]{2,1,0:T(8,128)(2,1)}), bf16[32,45,512]{2,1,0:T(8,128)(2,1)S(1)}, u32[]{:S(2)}, u32[]{:S(2)}) %all-to-all-start) | async-done | bytes 1474592 | tf_op jit(solution)/shard_map/all_to_all | solution.py:136
  75.3 1.4 copy.39
  76.7 47.7 %while.48 = (s32[]{:T(128)}, bf16[4,360,512]{2,1,0:T(8,128)(2,1)}, bf16[4,181]{1,0:T(4,128)(2,1)S(1)}, s32[4]{0:T(128)S(1)}, bf16[4,360,512]{2,1,0:T(8,128)(2,1)...) while((s32[]{:T(128)}, bf16[4,360,512]{2,1,0:T(8,128)(2,1)}, ...), condition=%wide.region_3.4_spmd, body=%wide.region_0.3_spmd.sunk | while | flops 37002472 | bytes 9913184 | solution.py:104
  80.5 7.2 %while.49 = (s32[]{:T(128)}, f32[8,45,512]{2,1,0:T(8,128)S(1)}, bf16[13,45,512]{2,1,0:T(8,128)(2,1)S(1)}, s32[]{:T(128)}, bf16[225]{0:T(256)(128)(2,1)S(1)}, /*i...) while((s32[]{:T(128)}, f32[8,45,512]{2,1,0:T(8,128)S(1)}, ...), condition=%wide.region_2.2_spmd.clone, body=%wide.region_1.1_spmd.clone.sunk | while | flops 35021032 | bytes 3736133 | solution.py:86
  92.4 7.2 %while.49 = (s32[]{:T(128)}, f32[8,45,512]{2,1,0:T(8,128)S(1)}, bf16[13,45,512]{2,1,0:T(8,128)(2,1)S(1)}, s32[]{:T(128)}, bf16[225]{0:T(256)(128)(2,1)S(1)}, /*i...) while((s32[]{:T(128)}, f32[8,45,512]{2,1,0:T(8,128)S(1)}, ...), condition=%wide.region_2.2_spmd.clone, body=%wide.region_1.1_spmd.clone.sunk | while | flops 35021032 | bytes 3736133 | solution.py:86
  104.3 7.2 %while.49 = (s32[]{:T(128)}, f32[8,45,512]{2,1,0:T(8,128)S(1)}, bf16[13,45,512]{2,1,0:T(8,128)(2,1)S(1)}, s32[]{:T(128)}, bf16[225]{0:T(256)(128)(2,1)S(1)}, /*i...) while((s32[]{:T(128)}, f32[8,45,512]{2,1,0:T(8,128)S(1)}, ...), condition=%wide.region_2.2_spmd.clone, body=%wide.region_1.1_spmd.clone.sunk | while | flops 35021032 | bytes 3736133 | solution.py:86
  116.2 7.2 %while.49 = (s32[]{:T(128)}, f32[8,45,512]{2,1,0:T(8,128)S(1)}, bf16[13,45,512]{2,1,0:T(8,128)(2,1)S(1)}, s32[]{:T(128)}, bf16[225]{0:T(256)(128)(2,1)S(1)}, /*i...) while((s32[]{:T(128)}, f32[8,45,512]{2,1,0:T(8,128)S(1)}, ...), condition=%wide.region_2.2_spmd.clone, body=%wide.region_1.1_spmd.clone.sunk | while | flops 35021032 | bytes 3736133 | solution.py:86
  124.4 3.2 %copy.40 = bf16[4,360,512]{2,0,1:T(4,128)(2,1)} copy(bf16[4,360,512]{2,1,0:T(8,128)(2,1)} %get-tuple-element.214) | data formatting | bytes 2949120 | tf_op jit(solution)/shard_map/while | solution.py:104
  127.6 3.8 %all-to-all-start.1 = ((bf16[4,360,512]{2,0,1:T(4,128)(2,1)}), bf16[4,360,512]{2,0,1:T(4,128)(2,1)S(1)}, u32[]{:S(2)}, u32[]{:S(2)}) async-start(bf16[4,360,512]{2,0,1:T(4,128)(2,1)} %copy.40), calls=%async_computation.1 | async-start | bytes 2949120 | tf_op jit(solution)/shard_map/all_to_all | solution.py:142
  131.4 3.0 %reshape.98 = f32[1440,512]{1,0:T(8,128)} reshape(bf16[32,45,512]{2,1,0:T(8,128)(2,1)} %get-tuple-element.274) | data formatting | bytes 4423680 | tf_op jit(solution)/shard_map/convert_element_type | solution.py:143
  134.4 16.6 %all-to-all-done.1 = bf16[4,360,512]{2,0,1:T(4,128)(2,1)S(1)} async-done(((bf16[4,360,512]{2,0,1:T(4,128)(2,1)}), bf16[4,360,512]{2,0,1:T(4,128)(2,1)S(1)}, u32[]{:S(2)}, u32[]{:S(2)}) %all-to-all-start.1) | async-done | bytes 1474592 | tf_op jit(solution)/shard_map/all_to_all | solution.py:142
  151.5 2.5 %copy.41 = f32[8,4,45,512]{3,2,1,0:T(8,128)} copy(f32[8,4,45,512]{3,1,2,0:T(4,128)S(1)} %convert_bitcast_fusion) | data formatting | bytes 5898240 | tf_op jit(solution)/shard_map/convert_element_type | solution.py:150
  154.0 3.4 %reshape.99 = f32[1440,512]{1,0:T(8,128)} reshape(f32[8,4,45,512]{3,2,1,0:T(8,128)} %copy.41) | data formatting | bytes 5898240 | tf_op jit(solution)/shard_map/convert_element_type | solution.py:150
  157.4 7.4 %fusion.25 = bf16[1440,512]{1,0:T(8,128)(2,1)} fusion(bf16[1024,512]{1,0:T(8,128)(2,1)S(1)} %copy-done, f32[1440,512]{1,0:T(8,128)} %reshape.98, f32[1440,512]{1,0:T(8,128)} %reshape.99, bf16[512,1024]{1,0:T(8,128)(2,1)S(1)} %copy-done.5, f32[512]{0:T(512)S(1)} %copy-done.6, f32[1440]{0:T(1024)S(1)} %rsqrt.12), kind=kOutput, calls=%fused_computation.41 | convolution fusion | flops 3037593600 | bytes 9477760 | tf_op jit(solution)/shard_map/dot_general | solution.py:149
  164.8 1.6 reshape.97
  166.4 1.9 %copy.44 = bf16[32,45,512]{2,0,1:T(8,128)(2,1)} copy(bf16[32,45,512]{2,1,0:T(8,128)(2,1)S(1)} %reshape.97) | data formatting | bytes 2949120 | tf_op jit(solution)/shard_map/reshape | solution.py:151
  (235 shorter events, 52.8 us)
Async XLA Ops:
  0.0 157.4 %copy-start = (bf16[1024,512]{1,0:T(8,128)(2,1)S(1)}, bf16[1024,512]{1,0:T(8,128)(2,1)}, u32[]{:S(2)}) copy-start(bf16[1024,512]{1,0:T(8,128)(2,1)} %param.21) | copy-start | bytes 3145732
  0.0 11.5 %copy-start.3 = (f32[9,512]{1,0:T(8,128)S(1)}, f32[9,512]{1,0:T(8,128)}, u32[]{:S(2)}) copy-start(f32[9,512]{1,0:T(8,128)} %param.15) | copy-start | bytes 55300
  2.5 5.4 %collective-permute-start = (bf16[32,1,512]{2,1,0:T(2,128)(2,1)S(1)}, bf16[32,1,512]{2,1,0:T(2,128)(2,1)S(1)}, u32[]{:S(2)}, u32[]{:S(2)}) collective-permute-start(bf16[32,1,512]{2,1,0:T(2,128)(2,1)S(1)} %get-tuple-element.287), channel_id=1, source_target_pairs={{0,1},{1,2},{2,3},{3,4},{4,5},{5,6},{6,7},{7,0},{8,9},{9,10},{10,1... | collective-permute-start | bytes 98312 | tf_op jit(solution)/shard_map/ppermute | solution.py:15
  3.0 4.8 %collective-permute-start.1 = (bf16[32,1,512]{2,1,0:T(2,128)(2,1)S(1)}, bf16[32,1,512]{2,1,0:T(2,128)(2,1)S(1)}, u32[]{:S(2)}, u32[]{:S(2)}) collective-permute-start(bf16[32,1,512]{2,1,0:T(2,128)(2,1)S(1)} %get-tuple-element.288), channel_id=1, source_target_pairs={{1,0},{2,1},{3,2},{4,3},{5,4},{6,5},{7,6},{0,7},{9,8},{10,9},{11,1... | collective-permute-start | bytes 98312 | tf_op jit(solution)/shard_map/ppermute | solution.py:17
  7.9 12.1 %copy-start.2 = (f32[32,45]{1,0:T(8,128)S(1)}, f32[32,45]{1,0:T(8,128)}, u32[]{:S(2)}) copy-start(f32[32,45]{1,0:T(8,128)} %param.14) | copy-start | bytes 17284
  7.9 8.3 %collective-permute-start.4 = (bf16[1,47,512]{2,1,0:T(8,128)(2,1)S(1)}, bf16[1,47,512]{2,1,0:T(8,128)(2,1)S(1)}, u32[]{:S(2)}, u32[]{:S(2)}) collective-permute-start(bf16[1,47,512]{2,1,0:T(8,128)(2,1)S(1)} %get-tuple-element.284), channel_id=1, source_target_pairs={{0,4},{1,5},{2,6},{3,7},{4,0},{5,1},{6,2},{7,3},{8,12},{9,13},{10,... | collective-permute-start | bytes 144392 | tf_op jit(solution)/shard_map/ppermute | solution.py:27
  10.3 6.0 %collective-permute-start.5 = (bf16[1,47,512]{2,1,0:T(8,128)(2,1)S(1)}, bf16[1,47,512]{2,1,0:T(8,128)(2,1)S(1)}, u32[]{:S(2)}, u32[]{:S(2)}) collective-permute-start(bf16[1,47,512]{2,1,0:T(8,128)(2,1)S(1)} %get-tuple-element.283), channel_id=1, source_target_pairs={{8,0},{16,8},{24,16},{9,1},{17,9},{25,17},{10,2},{18,10},{26,18},{... | collective-permute-start | bytes 144392 | tf_op jit(solution)/shard_map/ppermute | solution.py:17
  11.6 4.7 %collective-permute-start.2 = (bf16[1,47,512]{2,1,0:T(8,128)(2,1)S(1)}, bf16[1,47,512]{2,1,0:T(8,128)(2,1)S(1)}, u32[]{:S(2)}, u32[]{:S(2)}) collective-permute-start(bf16[1,47,512]{2,1,0:T(8,128)(2,1)S(1)} %get-tuple-element.283), channel_id=1, source_target_pairs={{0,4},{1,5},{2,6},{3,7},{4,0},{5,1},{6,2},{7,3},{8,12},{9,13},{10,... | collective-permute-start | bytes 144392 | tf_op jit(solution)/shard_map/ppermute | solution.py:27
  11.7 6.3 %collective-permute-start.3 = (bf16[1,47,512]{2,1,0:T(8,128)(2,1)S(1)}, bf16[1,47,512]{2,1,0:T(8,128)(2,1)S(1)}, u32[]{:S(2)}, u32[]{:S(2)}) collective-permute-start(bf16[1,47,512]{2,1,0:T(8,128)(2,1)S(1)} %get-tuple-element.284), channel_id=1, source_target_pairs={{0,8},{8,16},{16,24},{1,9},{9,17},{17,25},{2,10},{10,18},{18,26},{... | collective-permute-start | bytes 144392 | tf_op jit(solution)/shard_map/ppermute | solution.py:15
  20.1 13.8 %copy-start.4 = (f32[9,512]{1,0:T(8,128)S(1)}, f32[9,512]{1,0:T(8,128)}, u32[]{:S(2)}) copy-start(f32[9,512]{1,0:T(8,128)} %param.16) | copy-start | bytes 55300
  25.2 4.6 %collective-permute-start.6 = (bf16[32,1,512]{2,1,0:T(2,128)(2,1)S(1)}, bf16[32,1,512]{2,1,0:T(2,128)(2,1)S(1)}, u32[]{:S(2)}, u32[]{:S(2)}) collective-permute-start(bf16[32,1,512]{2,1,0:T(2,128)(2,1)S(1)} %get-tuple-element.285), channel_id=1, source_target_pairs={{0,1},{1,2},{2,3},{3,4},{4,5},{5,6},{6,7},{7,0},{8,9},{9,10},{10,1... | collective-permute-start | bytes 98312 | tf_op jit(solution)/shard_map/ppermute | solution.py:15
  25.2 4.6 %collective-permute-start.7 = (bf16[32,1,512]{2,1,0:T(2,128)(2,1)S(1)}, bf16[32,1,512]{2,1,0:T(2,128)(2,1)S(1)}, u32[]{:S(2)}, u32[]{:S(2)}) collective-permute-start(bf16[32,1,512]{2,1,0:T(2,128)(2,1)S(1)} %get-tuple-element.286), channel_id=1, source_target_pairs={{1,0},{2,1},{3,2},{4,3},{5,4},{6,5},{7,6},{0,7},{9,8},{10,9},{11,1... | collective-permute-start | bytes 98312 | tf_op jit(solution)/shard_map/ppermute | solution.py:17
  29.9 12.9 %copy-start.1 = (bf16[32,45,512]{2,0,1:T(8,128)(2,1)S(1)}, bf16[32,45,512]{2,0,1:T(8,128)(2,1)}, u32[]{:S(2)}) copy-start(bf16[32,45,512]{2,0,1:T(8,128)(2,1)} %param.13) | copy-start | bytes 4423684
  29.9 9.1 %collective-permute-start.10 = (bf16[1,47,512]{2,1,0:T(8,128)(2,1)S(1)}, bf16[1,47,512]{2,1,0:T(8,128)(2,1)S(1)}, u32[]{:S(2)}, u32[]{:S(2)}) collective-permute-start(bf16[1,47,512]{2,1,0:T(8,128)(2,1)S(1)} %get-tuple-element.280), channel_id=1, source_target_pairs={{0,4},{1,5},{2,6},{3,7},{4,0},{5,1},{6,2},{7,3},{8,12},{9,13},{10,... | collective-permute-start | bytes 144392 | tf_op jit(solution)/shard_map/ppermute | solution.py:27
  32.5 6.4 %collective-permute-start.11 = (bf16[1,47,512]{2,1,0:T(8,128)(2,1)S(1)}, bf16[1,47,512]{2,1,0:T(8,128)(2,1)S(1)}, u32[]{:S(2)}, u32[]{:S(2)}) collective-permute-start(bf16[1,47,512]{2,1,0:T(8,128)(2,1)S(1)} %get-tuple-element.279), channel_id=1, source_target_pairs={{8,0},{16,8},{24,16},{9,1},{17,9},{25,17},{10,2},{18,10},{26,18},{... | collective-permute-start | bytes 144392 | tf_op jit(solution)/shard_map/ppermute | solution.py:17
  33.9 5.1 %collective-permute-start.8 = (bf16[1,47,512]{2,1,0:T(8,128)(2,1)S(1)}, bf16[1,47,512]{2,1,0:T(8,128)(2,1)S(1)}, u32[]{:S(2)}, u32[]{:S(2)}) collective-permute-start(bf16[1,47,512]{2,1,0:T(8,128)(2,1)S(1)} %get-tuple-element.279), channel_id=1, source_target_pairs={{0,4},{1,5},{2,6},{3,7},{4,0},{5,1},{6,2},{7,3},{8,12},{9,13},{10,... | collective-permute-start | bytes 144392 | tf_op jit(solution)/shard_map/ppermute | solution.py:27
  34.1 6.6 %collective-permute-start.9 = (bf16[1,47,512]{2,1,0:T(8,128)(2,1)S(1)}, bf16[1,47,512]{2,1,0:T(8,128)(2,1)S(1)}, u32[]{:S(2)}, u32[]{:S(2)}) collective-permute-start(bf16[1,47,512]{2,1,0:T(8,128)(2,1)S(1)} %get-tuple-element.280), channel_id=1, source_target_pairs={{0,8},{8,16},{16,24},{1,9},{9,17},{17,25},{2,10},{10,18},{18,26},{... | collective-permute-start | bytes 144392 | tf_op jit(solution)/shard_map/ppermute | solution.py:15
  49.5 3.7 %copy-start.7 = (s32[32]{0:T(128)S(1)}, s32[32]{0:T(128)}, u32[]{:S(2)}) copy-start(s32[32]{0:T(128)} %param.17) | copy-start | bytes 388
  49.5 24.6 %all-to-all-start = ((bf16[32,45,512]{2,1,0:T(8,128)(2,1)}), bf16[32,45,512]{2,1,0:T(8,128)(2,1)S(1)}, u32[]{:S(2)}, u32[]{:S(2)}) async-start(bf16[32,45,512]{2,1,0:T(8,128)(2,1)} %get-tuple-element.274), calls=%async_computation | async-start | bytes 3145728 | tf_op jit(solution)/shard_map/all_to_all | solution.py:136
  127.6 23.5 %all-to-all-start.1 = ((bf16[4,360,512]{2,0,1:T(4,128)(2,1)}), bf16[4,360,512]{2,0,1:T(4,128)(2,1)S(1)}, u32[]{:S(2)}, u32[]{:S(2)}) async-start(bf16[4,360,512]{2,0,1:T(4,128)(2,1)} %copy.40), calls=%async_computation.1 | async-start | bytes 2949120 | tf_op jit(solution)/shard_map/all_to_all | solution.py:142
  154.0 3.4 %copy-start.5 = (bf16[512,1024]{1,0:T(8,128)(2,1)S(1)}, bf16[512,1024]{1,0:T(8,128)(2,1)}, u32[]{:S(2)}) copy-start(bf16[512,1024]{1,0:T(8,128)(2,1)} %param.20) | copy-start | bytes 3145732
  154.0 3.4 %copy-start.6 = (f32[512]{0:T(512)S(1)}, f32[512]{0:T(512)}, u32[]{:S(2)}) copy-start(f32[512]{0:T(512)} %param.19) | copy-start | bytes 6148
where the time goes:
time: 169 us; the launch traced here: 168 us
  local copies, waits for them, and re-layouts  44.2 us (26%)
  waiting for transfers between devices  44 us (26%)
  other arithmetic  32.3 us (19%)
  starting transfers between devices  30.9 us (18%)
  matrix products  15.4 us (9%)
    all_to_all x1, waiting for transfers between devices, local(): lax.all_to_all(mixed, 'lon', split_axis=0, concat_axis=1, tiled=True)  20.1 us
    all_to_all x1, waiting for transfers between devices, local(): lax.all_to_all(filtered, 'lon', split_axis=1, concat_axis=0, tiled=True)  16.6 us
    select_n x20, other arithmetic, tap_matrix(): segment = jnp.where(keep, segment, jnp.zeros_like(segment))  12.9 us
    ppermute x4, starting transfers between devices, padded_2(): lax.ppermute(tail, axis, [(i, (i + 1) % count) for i in range(ends)])  10 us
    ppermute x4, starting transfers between devices, padded_2(): lax.ppermute(head, axis, [((i + 1) % count, i) for i in range(ends)])  8.13 us
    dot_general x20, matrix products, add_block(): jnp.einsum('ab,pbc->pac', matrix, window, preferred_element_type=jnp.floa...  7.96 us
    dot_general x1, matrix products, local(): pointwise = jnp.dot(hidden, weight_out, preferred_element_type=jnp.float32)  7.4 us
    ppermute x4, waiting for transfers between devices, padded_2(): lax.ppermute(tail, axis, [(i, (i + 1) % count) for i in range(ends)])  7.19 us
  transfers between devices with their start and end apart: 14, of which 6 were waited for; matrix products, arithmetic and copies ran while one was open for 2% of the time, Pallas kernels for 0%

commit v1 on v0

v1 whole, which is shorter than its diff:
```python
import functools

import jax
import jax.numpy as jnp
from jax import lax
from jax.experimental import pallas as pl
from jax.experimental.pallas import tpu as pltpu
from jax.sharding import PartitionSpec as P

MESH = pl.DeviceIdType.MESH
LANES = 128
LEAD = 8


def round_up(value, step):
    return -(-value // step) * step


def gelu_tanh(values):
    return jax.nn.gelu(values, approximate=True)


def body(
    lats, n, rows, cols, chans, pad, reach,
    x_ref, metric_ref, tb_ref, lr_ref, k1_ref, k2_ref, gains_ref, gain_ref, win_ref, wout_ref,
    out_ref,
    ext, sec, held, acc, mix, circ, zsend, zrecv, side, taps,
    hs_sem, hr_sem, fs_sem, fr_sem, rs_sem, rr_sem,
):
    lat = lax.axis_index("lat")
    me = lax.axis_index("lon")
    chunks = rows // n
    half = n // 2
    wide = ext.shape[1]
    full = ext.shape[2]
    slabs = 2 * reach + 1

    at_top = lat == 0
    at_bottom = lat == lats - 1
    up_lat = jnp.where(at_top, 0, lat - 1)
    up_lon = jnp.where(at_top, lax.rem(me + half, n), me)
    down_lat = jnp.where(at_bottom, lats - 1, lat + 1)
    down_lon = jnp.where(at_bottom, lax.rem(me + half, n), me)
    left = lax.rem(me + n - 1, n)
    right = lax.rem(me + 1, n)

    def before(lon):
        return lax.rem(lon + n - 1, n)

    def after(lon):
        return lax.rem(lon + 1, n)

    def clear(e, carry):
        ext[e, 0:LEAD, :] = jnp.zeros((LEAD, full), jnp.float32)
        return carry

    lax.fori_loop(0, rows + 4, clear, 0)

    barrier = pltpu.get_barrier_semaphore()
    greeted = [
        (lat, left), (lat, right),
        (up_lat, up_lon), (up_lat, before(up_lon)), (up_lat, after(up_lon)),
        (down_lat, down_lon), (down_lat, before(down_lon)), (down_lat, after(down_lon)),
    ] + [(lat, lax.rem(me + o, n)) for o in range(1, n)]
    for device in greeted:
        pl.semaphore_signal(barrier, inc=1, device_id=device, device_id_type=MESH)
    pl.semaphore_wait(barrier, len(greeted))

    halo = []

    def send_halo(src, dst, recv_index, device):
        copy = pltpu.make_async_remote_copy(
            src_ref=src, dst_ref=dst, send_sem=hs_sem.at[len(halo)], recv_sem=hr_sem.at[recv_index],
            device_id=device, device_id_type=MESH,
        )
        copy.start()
        halo.append(copy)

    def slot_row(slot):
        return jnp.where(slot < 2, slot, rows + slot)

    send_halo(lr_ref.at[0], side.at[1, pl.ds(2, rows)], 5, (lat, left))
    send_halo(lr_ref.at[1], side.at[0, pl.ds(2, rows)], 4, (lat, right))
    for i in range(2):
        up_slot = jnp.where(at_top, 1 - i, 2 + i)
        down_slot = jnp.where(at_bottom, 3 - i, i)
        for slot, src_row, device_lat, device_lon in (
            (up_slot, i, up_lat, up_lon),
            (down_slot, rows - 2 + i, down_lat, down_lon),
        ):
            tb = i if src_row < 2 else 2 + i
            dst_row = slot_row(slot)
            send_halo(
                tb_ref.at[tb], ext.at[dst_row, pl.ds(LEAD, pad)], slot, (device_lat, device_lon)
            )
            send_halo(
                lr_ref.at[0, src_row], side.at[1, dst_row], 10 + slot,
                (device_lat, before(device_lon)),
            )
            send_halo(
                lr_ref.at[1, src_row], side.at[0, dst_row], 6 + slot,
                (device_lat, after(device_lon)),
            )

    def place(i, carry):
        weight = metric_ref[i]
        ext[i + 2, pad:wide, :] = jnp.zeros((wide - pad, full), jnp.float32)
        held[i, pad - 8:pad, :] = jnp.zeros((8, chans), jnp.float32)
        ext[i + 2, LEAD:LEAD + cols, chans:] = weight
        for c in range(chans // LANES):
            lanes = slice(c * LANES, (c + 1) * LANES)
            cells = x_ref[i, :, lanes].astype(jnp.float32)
            held[i, 0:cols, lanes] = cells
            ext[i + 2, LEAD:LEAD + cols, lanes] = (
                (cells * weight).astype(jnp.bfloat16).astype(jnp.float32)
            )
        return carry

    lax.fori_loop(0, rows, place, 0)

    tap_lanes = taps.shape[2]
    lane_ids = lax.broadcasted_iota(jnp.int32, (pad, tap_lanes), 1)
    for k in range(chunks):
        line = jnp.broadcast_to(gains_ref[pl.ds(k * n + me, 1), :], (pad, tap_lanes))
        shifted = pltpu.roll(line, 0, 1, stride=1, stride_axis=0)
        total = jnp.zeros((pad, tap_lanes), jnp.float32)
        for d in range(slabs):
            moved = pltpu.roll(shifted, (pad - cols) * d, 1) if d else shifted
            inside = (lane_ids >= pad * d) & (lane_ids < pad * d + cols)
            total = jnp.where(inside, moved, total)
        taps[k] = total.astype(jnp.bfloat16)

    def recv_halo(src, dst, recv_index):
        pltpu.make_async_remote_copy(
            src_ref=src, dst_ref=dst, send_sem=hs_sem.at[0], recv_sem=hr_sem.at[recv_index],
            device_id=(lat, right), device_id_type=MESH,
        ).wait_recv()

    for s in range(2):
        recv_halo(lr_ref.at[s], side.at[s, pl.ds(2, rows)], 4 + s)
    for slot in range(4):
        row = slot if slot < 2 else rows + slot
        recv_halo(tb_ref.at[0], ext.at[row, pl.ds(LEAD, pad)], slot)
        for s in range(2):
            recv_halo(lr_ref.at[0, 0], side.at[s, row], 6 + 4 * s + slot)

    def join(e, carry):
        ext[e, LEAD - 2:LEAD, :] = side[0, e]
        ext[e, LEAD + cols:LEAD + cols + 2, :] = side[1, e]
        return carry

    lax.fori_loop(0, rows + 4, join, 0)

    def stencil(src, row, kernel, lanes):
        sums = [None, None, None]
        for a in range(3):
            line = src[row + a, :, lanes]
            for b in range(3):
                term = kernel(3 * a + b, lanes) * line
                sums[b] = term if sums[b] is None else sums[b] + term
        return pltpu.roll(sums[0], 1, 0) + sums[1] + pltpu.roll(sums[2], wide - 1, 0)

    def second_row(p, carry):
        flip = ((p == 0) & at_top) | ((p == rows + 1) & at_bottom)
        which = jnp.where(flip, 1, 0)
        weight = ext[p + 1, :, chans:]
        for c in range(chans // LANES):
            lanes = slice(c * LANES, (c + 1) * LANES)
            value = stencil(ext, p, lambda t, l: k1_ref[which, t:t + 1, l], lanes)
            value = weight * gelu_tanh(value)
            sec[p, :, lanes] = value.astype(jnp.bfloat16).astype(jnp.float32)
        return carry

    col_ids = lax.broadcasted_iota(jnp.int32, (pad, LANES), 0)

    def mixed_row(i, carry):
        for c in range(chans // LANES):
            lanes = slice(c * LANES, (c + 1) * LANES)
            value = stencil(sec, i, lambda t, l: k2_ref[t:t + 1, l], lanes)
            value = held[i, :, lanes] + value[LEAD:, :]
            mix[i, :, lanes] = jnp.where(col_ids < cols, value, 0.0).astype(jnp.bfloat16)
        return carry

    forward = []
    for k in range(chunks):
        start = 0 if k == 0 else k * n + 2
        lax.fori_loop(start, (k + 1) * n + 2, second_row, 0)
        lax.fori_loop(k * n, (k + 1) * n, mixed_row, 0)
        for o in range(1, n):
            target = lax.rem(me + o, n)
            copy = pltpu.make_async_remote_copy(
                src_ref=mix.at[k * n + target], dst_ref=circ.at[k, me + reach],
                send_sem=fs_sem.at[k, o], recv_sem=fr_sem.at[k, o],
                device_id=(lat, target), device_id_type=MESH,
            )
            copy.start()
            forward.append(copy)
        circ[k, me + reach] = mix[k * n + me]

    group = 8

    def network(g, carry):
        flat = mix[pl.ds(g * group, group)].reshape(group * pad, chans).astype(jnp.float32)
        scale = lax.rsqrt(jnp.mean(flat * flat, axis=1, keepdims=True) + 1e-06)
        normed = (flat * scale * gain_ref[...]).astype(jnp.bfloat16)
        hidden = gelu_tanh(
            jnp.dot(normed, win_ref[...], preferred_element_type=jnp.float32)
        ).astype(jnp.bfloat16)
        point = jnp.dot(hidden, wout_ref[...], preferred_element_type=jnp.float32)
        acc[pl.ds(g * group, group)] = (flat + point).reshape(group, pad, chans)
        return carry

    lax.fori_loop(0, rows // group, network, 0)

    back = []
    for k in range(chunks):
        for o in range(1, n):
            source = lax.rem(me + n - o, n)
            pltpu.make_async_remote_copy(
                src_ref=mix.at[k * n], dst_ref=circ.at[k, source + reach],
                send_sem=fs_sem.at[k, o], recv_sem=fr_sem.at[k, o],
                device_id=(lat, source), device_id_type=MESH,
            ).wait_recv()
        for e in range(reach):
            circ[k, e] = circ[k, n + e]
            circ[k, n + reach + e] = circ[k, reach + e]

        def filter_block(a, carry):
            window = circ[k, pl.ds(a, slabs)].reshape(slabs * pad, chans)
            result = jnp.dot(
                taps[k, :, 0:slabs * pad], window, preferred_element_type=jnp.float32
            )
            zsend[k * n + a] = result.astype(jnp.bfloat16)
            return carry

        lax.fori_loop(0, n, filter_block, 0, unroll=4)
        for o in range(1, n):
            target = lax.rem(me + o, n)
            copy = pltpu.make_async_remote_copy(
                src_ref=zsend.at[k * n + target], dst_ref=zrecv.at[k * n + me],
                send_sem=rs_sem.at[k, o], recv_sem=rr_sem.at[k, o],
                device_id=(lat, target), device_id_type=MESH,
            )
            copy.start()
            back.append(copy)
        zrecv[k * n + me] = zsend[k * n + me]

    for k in range(chunks):
        for o in range(1, n):
            source = lax.rem(me + n - o, n)
            pltpu.make_async_remote_copy(
                src_ref=zsend.at[k * n], dst_ref=zrecv.at[k * n + source],
                send_sem=rs_sem.at[k, o], recv_sem=rr_sem.at[k, o],
                device_id=(lat, source), device_id_type=MESH,
            ).wait_recv()

        def finish(i, carry):
            out_ref[i] = (acc[i] + zrecv[i].astype(jnp.float32)).astype(jnp.bfloat16)
            return carry

        lax.fori_loop(k * n, (k + 1) * n, finish, 0)

    for copy in halo + forward + back:
        copy.wait_send()


def local(
    lats, n,
    inputs, metric, kernel_one, kernel_two, widths, zonal_gains, norm_gain, weight_in, weight_out
):
    rows, cols, chans = inputs.shape
    pad = round_up(cols, 16)
    wide = LEAD + pad
    full = chans + LANES
    reach = n // 4
    slabs = 2 * reach + 1
    count = zonal_gains.shape[1]
    center = (count - 1) // 2
    tap_lanes = round_up(max(slabs * pad, count + pad - 1), LANES)

    def packed(cells, weights):
        weights = weights[:, :, None]
        first = (cells.astype(jnp.float32) * weights).astype(jnp.bfloat16).astype(jnp.float32)
        spread = jnp.broadcast_to(weights, weights.shape[:2] + (LANES,))
        return jnp.concatenate([first, spread], axis=2)

    spread = jnp.broadcast_to(metric[:, :, None], (rows, cols, LANES))
    edge_cells = jnp.concatenate([inputs[:2], inputs[-2:]], axis=0)
    edge_weights = jnp.concatenate([metric[:2], metric[-2:]], axis=0)
    tb = jnp.pad(packed(edge_cells, edge_weights), ((0, 0), (0, pad - cols), (0, 0)))
    lr = jnp.stack(
        [packed(inputs[:, :2], metric[:, :2]), packed(inputs[:, -2:], metric[:, -2:])]
    )
    flipped = kernel_one.reshape(3, 3, chans)[::-1].reshape(9, chans)
    k_one = jnp.stack([kernel_one, flipped])
    offsets = jnp.abs(jnp.arange(count, dtype=jnp.int32) - center)
    kept = jnp.where(
        offsets[None, :] <= widths[:, None], zonal_gains.astype(jnp.float32), 0.0
    )
    kept = jnp.pad(kept, ((0, 0), (0, tap_lanes - count)))
    chunks = rows // n
    vmem = pl.BlockSpec(memory_space=pltpu.VMEM)
    sem = pltpu.SemaphoreType.DMA
    out = pl.pallas_call(
        functools.partial(body, lats, n, rows, cols, chans, pad, reach),
        out_shape=jax.ShapeDtypeStruct((rows, pad, chans), jnp.bfloat16),
        in_specs=[vmem] * 10,
        out_specs=vmem,
        scratch_shapes=[
            pltpu.VMEM((rows + 4, wide, full), jnp.float32),
            pltpu.VMEM((rows + 2, wide, chans), jnp.float32),
            pltpu.VMEM((rows, pad, chans), jnp.float32),
            pltpu.VMEM((rows, pad, chans), jnp.float32),
            pltpu.VMEM((rows, pad, chans), jnp.bfloat16),
            pltpu.VMEM((chunks, n + 2 * reach, pad, chans), jnp.bfloat16),
            pltpu.VMEM((rows, pad, chans), jnp.bfloat16),
            pltpu.VMEM((rows, pad, chans), jnp.bfloat16),
            pltpu.VMEM((2, rows + 4, 2, full), jnp.float32),
            pltpu.VMEM((chunks, pad, tap_lanes), jnp.bfloat16),
            sem((14,)), sem((14,)),
            sem((chunks, n)), sem((chunks, n)), sem((chunks, n)), sem((chunks, n)),
        ],
        compiler_params=pltpu.CompilerParams(
            collective_id=0, has_side_effects=True, vmem_limit_bytes=60 * 2**20
        ),
    )(
        inputs, spread, tb, lr, k_one, kernel_two, kept, norm_gain.reshape(1, chans),
        weight_in, weight_out,
    )
    return out[:, :cols]


def solution(mesh):
    placed = (
        P("lat", "lon", None),
        P("lat", "lon"),
        P(),
        P(),
        P("lat"),
        P("lat", None),
        P(),
        P(),
        P(),
    )
    return jax.shard_map(
        functools.partial(local, mesh.shape["lat"], mesh.shape["lon"]),
        mesh=mesh, in_specs=placed, out_specs=P("lat", "lon", None), check_vma=False,
    )
```

time: 169 us -> 71.3 us (0.42)
  Pallas kernels: 0 us -> 56.8 us
  waiting for transfers between devices: 44 us -> 0 us
  local copies, waits for them, and re-layouts: 44.2 us -> 9.41 us
  starting transfers between devices: 30.9 us -> 0 us
  other arithmetic: 32.3 us -> 4.47 us
  matrix products: 15.4 us -> 0 us
    pallas_call x0 -> x1, Pallas kernels: none -> 56.8 us  [local(): pl.pallas_call(functools.partial(body, lats, n, rows, cols, chans, pad, r...]
    all_to_all x2 -> x0, waiting for transfers between devices: 36.8 us -> none  [the longest x1 20.1 us: local(): lax.all_to_all(mixed, 'lon', split_axis=0, concat_axis=1, tiled=True)]
    ppermute x12 -> x0, starting transfers between devices: 23.5 us -> none  [the longest x4 10 us: padded_2(): lax.ppermute(tail, axis, [(i, (i + 1) % count) for i in range(ends)])]
    dot_general x21 -> x0, matrix products: 15.4 us -> none  [the longest x20 7.96 us: add_block(): jnp.einsum('ab,pbc->pac', matrix, window, preferred_element_type=jnp.floa...]
    select_n x24 -> x1, other arithmetic: 12.9 us -> 0.79 us  [local(): jnp.where(offsets[None, :] <= widths[:, None], zonal_gains.astype(jnp.flo...]
    convert_element_type x7 -> x0, local copies, waits for them, and re-layouts: 9.35 us -> none  [the longest x2 5.9 us: local(): zonal.reshape(-1, channels).astype(jnp.float32)]
    convert_element_type x7 -> x2, other arithmetic: 7.96 us -> 0.25 us  [packed(): (cells.astype(jnp.float32) * weights).astype(jnp.bfloat16)]
    all_to_all x2 -> x0, starting transfers between devices: 7.47 us -> none  [the longest x1 3.76 us: local(): lax.all_to_all(filtered, 'lon', split_axis=1, concat_axis=0, tiled=True)]
  transfers between devices with their start and end apart: 14 -> 0, of which waited for: 6 -> 0; matrix products, arithmetic and copies ran while one was open for 2% -> 0% of each run, Pallas kernels for 0% -> 0%
where the time goes in v1:
time: 71.3 us; the launch traced here: 70.8 us
  Pallas kernels  56.8 us (80%)
  local copies, waits for them, and re-layouts  9.41 us (13%)
  other arithmetic  4.47 us (6%)
    pallas_call x1, Pallas kernels, local(): pl.pallas_call(functools.partial(body, lats, n, rows, cols, chans, pad, r...  56.8 us
    slice x1, local copies, waits for them, and re-layouts, local(): return out[:, :cols]  3.35 us
    broadcast_in_dim x1, local copies, waits for them, and re-layouts, local(): spread = jnp.broadcast_to(metric[:, :, None], (rows, cols, LANES))  1.87 us

profile of v1, /device:TPU:0, one launch (start us, length us, event | category | flops | bytes accessed | tf_op | source)
XLA Modules:
  0.0 70.8 jit_solution(14441058513802071179)
XLA Ops:
  0.0 0.0 copy-start.1
  0.0 0.8 %fusion.5 = (f32[2,45]{1,0:T(2,128)S(1)}, f32[2,45]{1,0:T(2,128)S(1)}) fusion(f32[32,45]{1,0:T(8,128)} %param.10), kind=kLoop, calls=%fused_computation.17 | loop fusion | bytes 1440 | tf_op jit(solution)/shard_map/slice | solution.py:289
  0.8 0.8 %reshape.16 = f32[3,3,512]{2,1,0:T(4,128)S(1)} reshape(f32[9,512]{1,0:T(8,128)} %param.11) | data formatting | bytes 36864 | tf_op jit(solution)/shard_map/reshape | solution.py:294
  1.6 0.8 %convert_select_fusion = f32[32,181]{1,0:T(8,128)S(1)} fusion(bf16[32,181]{1,0:T(8,128)(2,1)} %param.14, s32[181]{0:T(256)S(1)} %add_abs_fusion, s32[32]{0:T(128)} %param.13), kind=kLoop, calls=%fused_computation.12 | loop fusion | flops 17376 | bytes 35604 | tf_op jit(solution)/shard_map/jit(_where)/select_n | solution.py:297
  2.4 0.6 pad.9.gains_ref
  3.1 1.4 %pad_maximum_fusion.1.k1_ref = f32[2,9,512]{2,1,0:T(8,128)} fusion(f32[1,9,512]{2,1,0:T(8,128)S(1)} %stack_reshape.3, f32[1,9,512]{2,1,0:T(8,128)} %bitcast.8), kind=kLoop, calls=%fused_computation.11 | loop fusion | flops 9216 | bytes 73728 | tf_op jit(solution)/shard_map/stack | solution.py:295
  4.5 0.9 %fusion.4 = (f32[32,2]{1,0:T(8,128)S(1)}, f32[32,2]{1,0:T(8,128)S(1)}) fusion(f32[32,45]{1,0:T(8,128)} %param.10), kind=kLoop, calls=%fused_computation.16 | loop fusion | bytes 1024 | tf_op jit(solution)/shard_map/slice | solution.py:292
  5.3 0.1 broadcast_in_dim.13
  5.4 0.1 broadcast_in_dim.14
  5.5 0.1 broadcast_in_dim.12
  5.6 1.9 %broadcast_in_dim.11.metric_ref = f32[32,45,128]{2,1,0:T(8,128)} broadcast(f32[32,45]{1,0:T(8,128)} %param.10), dimensions={0,1} | broadcast | bytes 743040 | tf_op jit(solution)/shard_map/broadcast_in_dim | solution.py:287
  7.5 0.0 copy-done.1
  7.5 0.8 %copy.20.x_ref = bf16[32,45,512]{2,1,0:T(8,128)(2,1)S(1)} copy(bf16[32,45,512]{2,0,1:T(8,128)(2,1)S(1)} %copy-done.1) | data formatting | bytes 2949120 | tf_op args[0]
  8.3 0.0 copy-start
  8.3 0.1 fusion
  8.4 1.0 %select_maximum_fusion.tb_ref = f32[4,48,640]{2,1,0:T(8,128)} fusion(f32[4,45,128]{2,1,0:T(8,128)S(1)} %broadcast_in_dim.12, f32[4,45,512]{2,1,0:T(8,128)S(1)} %fusion), kind=kLoop, calls=%fused_computation | loop fusion | flops 491520 | bytes 952320 | tf_op jit(solution)/shard_map/concatenate | solution.py:285
  9.4 0.2 fusion.1
  9.6 0.2 maximum_bitcast_fusion
  9.7 0.9 %pad_maximum_fusion.lr_ref = f32[2,32,2,640]{3,2,1,0:T(2,128)} fusion(f32[1,32,2,640]{3,2,1,0:T(2,128)S(1)} %get-tuple-element.14, f32[1,32,2,640]{3,2,1,0:T(2,128)S(1)} %get-tuple-element.13), kind=kLoop, calls=%fused_computation.3 | loop fusion | flops 81920 | bytes 655360 | tf_op jit(solution)/shard_map/stack | solution.py:291
  10.6 0.0 copy-done
  10.6 56.8 %shard_map.91 = bf16[32,48,512]{2,1,0:T(8,128)(2,1)} custom-call(bf16[32,45,512]{2,1,0:T(8,128)(2,1)} %copy-done, f32[32,45,128]{2,1,0:T(8,128)} %broadcast_in_dim.11.metric_ref, f32[4,48,640]{2,1,0:T(8,128)} %select_maximum_fusion.tb_ref, f32[2,32,2,640]{3,2,1,0:T(2,128)} %pad_maximum_fusion.lr_ref, f32[2,9,512]{2,1,0:T(8,128)} %pad_maximum_fusion.1.k1_ref, ...), custom_call_target="tpu_custom_call" | custom-call | tf_op jit(solution)/shard_map/pallas_call | solution.py:304
  67.4 3.3 %copy.21 = bf16[32,45,512]{2,0,1:T(8,128)(2,1)} copy(bf16[32,45,512]{2,1,0:T(8,128)(2,1)} %bitcast.7) | data formatting | bytes 2949120 | tf_op jit(solution)/shard_map/slice | solution.py:330
  (5 shorter events, 0.1 us)
Async XLA Ops:
  0.0 7.5 %copy-start.1 = (bf16[32,45,512]{2,0,1:T(8,128)(2,1)S(1)}, bf16[32,45,512]{2,0,1:T(8,128)(2,1)}, u32[]{:S(2)}) copy-start(bf16[32,45,512]{2,0,1:T(8,128)(2,1)} %param.9) | copy-start | bytes 4423684
  8.3 2.3 %copy-start = (bf16[32,45,512]{2,1,0:T(8,128)(2,1)}, bf16[32,45,512]{2,1,0:T(8,128)(2,1)S(1)}, u32[]{:S(2)}) copy-start(bf16[32,45,512]{2,1,0:T(8,128)(2,1)S(1)} %copy.20.x_ref) | copy-start | bytes 4423684

commit v2 on v1

--- a/solution.py
+++ b/solution.py
@@ -22,9 +22,10 @@
 
 def body(
     lats, n, rows, cols, chans, pad, reach,
-    x_ref, metric_ref, tb_ref, lr_ref, k1_ref, k2_ref, gains_ref, gain_ref, win_ref, wout_ref,
+    x_ref, metric_ref, k1_ref, k2_ref, widths_ref, gains_ref, gain_ref, win_hbm, wout_hbm,
     out_ref,
-    ext, sec, held, acc, mix, circ, zsend, zrecv, side, taps,
+    ext, sec, held, acc, mix, circ, zsend, zrecv, lr_ref, side, taps, lines, taps_one, win_ref, wout_ref,
+    w_sem,
     hs_sem, hr_sem, fs_sem, fr_sem, rs_sem, rr_sem,
 ):
     lat = lax.axis_index("lat")
@@ -50,11 +51,12 @@
     def after(lon):
         return lax.rem(lon + 1, n)
 
-    def clear(e, carry):
-        ext[e, 0:LEAD, :] = jnp.zeros((LEAD, full), jnp.float32)
-        return carry
-
-    lax.fori_loop(0, rows + 4, clear, 0)
+    loads = [
+        pltpu.make_async_copy(win_hbm, win_ref, w_sem.at[0]),
+        pltpu.make_async_copy(wout_hbm, wout_ref, w_sem.at[1]),
+    ]
+    for load in loads:
+        load.start()
 
     barrier = pltpu.get_barrier_semaphore()
     greeted = [
@@ -64,6 +66,36 @@
     ] + [(lat, lax.rem(me + o, n)) for o in range(1, n)]
     for device in greeted:
         pl.semaphore_signal(barrier, inc=1, device_id=device, device_id_type=MESH)
+    def clear(e, carry):
+        ext[e, 0:LEAD, :] = jnp.zeros((LEAD, full), jnp.float32)
+        return carry
+
+    lax.fori_loop(0, rows + 4, clear, 0)
+
+    diagonal = lax.broadcasted_iota(jnp.int32, (pad, cols), 0) == lax.broadcasted_iota(
+        jnp.int32, (pad, cols), 1
+    )
+
+    def place(i, carry):
+        line = jnp.broadcast_to(metric_ref[pl.ds(i, 1), :], (pad, cols))
+        column = jnp.sum(jnp.where(diagonal, line, 0.0), axis=1, keepdims=True)
+        weight = jnp.broadcast_to(column, (pad, LANES))
+        ext[i + 2, pad:wide, :] = jnp.zeros((wide - pad, full), jnp.float32)
+        held[i, pad - 8:pad, :] = jnp.zeros((8, chans), jnp.float32)
+        ext[i + 2, LEAD:wide, chans:] = weight
+        lr_ref[0, i, :, chans:] = weight[0:2]
+        lr_ref[1, i, :, chans:] = weight[cols - 2:cols]
+        for c in range(chans // LANES):
+            lanes = slice(c * LANES, (c + 1) * LANES)
+            cells = x_ref[i, :, lanes].astype(jnp.float32)
+            held[i, 0:cols, lanes] = cells
+            first = (cells * weight[0:cols]).astype(jnp.bfloat16).astype(jnp.float32)
+            ext[i + 2, LEAD:LEAD + cols, lanes] = first
+            lr_ref[0, i, :, lanes] = first[0:2]
+            lr_ref[1, i, :, lanes] = first[cols - 2:cols]
+        return carry
+
+    lax.fori_loop(0, rows, place, 0)
     pl.semaphore_wait(barrier, len(greeted))
 
     halo = []
@@ -88,10 +120,9 @@
             (up_slot, i, up_lat, up_lon),
             (down_slot, rows - 2 + i, down_lat, down_lon),
         ):
-            tb = i if src_row < 2 else 2 + i
             dst_row = slot_row(slot)
             send_halo(
-                tb_ref.at[tb], ext.at[dst_row, pl.ds(LEAD, pad)], slot, (device_lat, device_lon)
+                ext.at[src_row + 2, pl.ds(LEAD, pad)], ext.at[dst_row, pl.ds(LEAD, pad)], slot, (device_lat, device_lon)
             )
             send_halo(
                 lr_ref.at[0, src_row], side.at[1, dst_row], 10 + slot,
@@ -102,26 +133,19 @@
                 (device_lat, after(device_lon)),
             )
 
-    def place(i, carry):
-        weight = metric_ref[i]
-        ext[i + 2, pad:wide, :] = jnp.zeros((wide - pad, full), jnp.float32)
-        held[i, pad - 8:pad, :] = jnp.zeros((8, chans), jnp.float32)
-        ext[i + 2, LEAD:LEAD + cols, chans:] = weight
-        for c in range(chans // LANES):
-            lanes = slice(c * LANES, (c + 1) * LANES)
-            cells = x_ref[i, :, lanes].astype(jnp.float32)
-            held[i, 0:cols, lanes] = cells
-            ext[i + 2, LEAD:LEAD + cols, lanes] = (
-                (cells * weight).astype(jnp.bfloat16).astype(jnp.float32)
-            )
-        return carry
-
-    lax.fori_loop(0, rows, place, 0)
-
     tap_lanes = taps.shape[2]
     lane_ids = lax.broadcasted_iota(jnp.int32, (pad, tap_lanes), 1)
+    taps_one[0, 0:9] = k1_ref[...]
+    for a in range(3):
+        taps_one[1, 3 * a:3 * a + 3] = k1_ref[6 - 3 * a:9 - 3 * a, :]
+    count = gains_ref.shape[1]
+    center = (count - 1) // 2
+    lines[...] = jnp.zeros(lines.shape, jnp.float32)
+    lines[:, 0:count] = gains_ref[...].astype(jnp.float32)
     for k in range(chunks):
-        line = jnp.broadcast_to(gains_ref[pl.ds(k * n + me, 1), :], (pad, tap_lanes))
+        line = jnp.broadcast_to(lines[pl.ds(k * n + me, 1), :], (pad, tap_lanes))
+        kept = jnp.abs(lane_ids - center) <= widths_ref[k * n + me]
+        line = jnp.where(kept, line, 0.0)
         shifted = pltpu.roll(line, 0, 1, stride=1, stride_axis=0)
         total = jnp.zeros((pad, tap_lanes), jnp.float32)
         for d in range(slabs):
@@ -140,9 +164,12 @@
         recv_halo(lr_ref.at[s], side.at[s, pl.ds(2, rows)], 4 + s)
     for slot in range(4):
         row = slot if slot < 2 else rows + slot
-        recv_halo(tb_ref.at[0], ext.at[row, pl.ds(LEAD, pad)], slot)
+        recv_halo(ext.at[2, pl.ds(LEAD, pad)], ext.at[row, pl.ds(LEAD, pad)], slot)
         for s in range(2):
             recv_halo(lr_ref.at[0, 0], side.at[s, row], 6 + 4 * s + slot)
+
+    for copy in halo:
+        copy.wait_send()
 
     def join(e, carry):
         ext[e, LEAD - 2:LEAD, :] = side[0, e]
@@ -156,7 +183,7 @@
         for a in range(3):
             line = src[row + a, :, lanes]
             for b in range(3):
-                term = kernel(3 * a + b, lanes) * line
+                term = kernel(a, b, lanes) * line
                 sums[b] = term if sums[b] is None else sums[b] + term
         return pltpu.roll(sums[0], 1, 0) + sums[1] + pltpu.roll(sums[2], wide - 1, 0)
 
@@ -166,7 +193,7 @@
         weight = ext[p + 1, :, chans:]
         for c in range(chans // LANES):
             lanes = slice(c * LANES, (c + 1) * LANES)
-            value = stencil(ext, p, lambda t, l: k1_ref[which, t:t + 1, l], lanes)
+            value = stencil(ext, p, lambda a, b, l: taps_one[which, 3 * a + b:3 * a + b + 1, l], lanes)
             value = weight * gelu_tanh(value)
             sec[p, :, lanes] = value.astype(jnp.bfloat16).astype(jnp.float32)
         return carry
@@ -176,7 +203,7 @@
     def mixed_row(i, carry):
         for c in range(chans // LANES):
             lanes = slice(c * LANES, (c + 1) * LANES)
-            value = stencil(sec, i, lambda t, l: k2_ref[t:t + 1, l], lanes)
+            value = stencil(sec, i, lambda a, b, l: k2_ref[3 * a + b:3 * a + b + 1, l], lanes)
             value = held[i, :, lanes] + value[LEAD:, :]
             mix[i, :, lanes] = jnp.where(col_ids < cols, value, 0.0).astype(jnp.bfloat16)
         return carry
@@ -196,6 +223,9 @@
             copy.start()
             forward.append(copy)
         circ[k, me + reach] = mix[k * n + me]
+
+    for load in loads:
+        load.wait()
 
     group = 8
 
@@ -260,7 +290,7 @@
 
         lax.fori_loop(k * n, (k + 1) * n, finish, 0)
 
-    for copy in halo + forward + back:
+    for copy in forward + back:
         copy.wait_send()
 
 
@@ -275,36 +305,17 @@
     reach = n // 4
     slabs = 2 * reach + 1
     count = zonal_gains.shape[1]
-    center = (count - 1) // 2
     tap_lanes = round_up(max(slabs * pad, count + pad - 1), LANES)
 
-    def packed(cells, weights):
-        weights = weights[:, :, None]
-        first = (cells.astype(jnp.float32) * weights).astype(jnp.bfloat16).astype(jnp.float32)
-        spread = jnp.broadcast_to(weights, weights.shape[:2] + (LANES,))
-        return jnp.concatenate([first, spread], axis=2)
-
-    spread = jnp.broadcast_to(metric[:, :, None], (rows, cols, LANES))
-    edge_cells = jnp.concatenate([inputs[:2], inputs[-2:]], axis=0)
-    edge_weights = jnp.concatenate([metric[:2], metric[-2:]], axis=0)
-    tb = jnp.pad(packed(edge_cells, edge_weights), ((0, 0), (0, pad - cols), (0, 0)))
-    lr = jnp.stack(
-        [packed(inputs[:, :2], metric[:, :2]), packed(inputs[:, -2:], metric[:, -2:])]
-    )
-    flipped = kernel_one.reshape(3, 3, chans)[::-1].reshape(9, chans)
-    k_one = jnp.stack([kernel_one, flipped])
-    offsets = jnp.abs(jnp.arange(count, dtype=jnp.int32) - center)
-    kept = jnp.where(
-        offsets[None, :] <= widths[:, None], zonal_gains.astype(jnp.float32), 0.0
-    )
-    kept = jnp.pad(kept, ((0, 0), (0, tap_lanes - count)))
     chunks = rows // n
     vmem = pl.BlockSpec(memory_space=pltpu.VMEM)
     sem = pltpu.SemaphoreType.DMA
     out = pl.pallas_call(
         functools.partial(body, lats, n, rows, cols, chans, pad, reach),
         out_shape=jax.ShapeDtypeStruct((rows, pad, chans), jnp.bfloat16),
-        in_specs=[vmem] * 10,
+        in_specs=[vmem] * 4
+        + [pl.BlockSpec(memory_space=pltpu.SMEM), vmem, vmem]
+        + [pl.BlockSpec(memory_space=pl.ANY)] * 2,
         out_specs=vmem,
         scratch_shapes=[
             pltpu.VMEM((rows + 4, wide, full), jnp.float32),
@@ -315,8 +326,14 @@
             pltpu.VMEM((chunks, n + 2 * reach, pad, chans), jnp.bfloat16),
             pltpu.VMEM((rows, pad, chans), jnp.bfloat16),
             pltpu.VMEM((rows, pad, chans), jnp.bfloat16),
+            pltpu.VMEM((2, rows, 2, full), jnp.float32),
             pltpu.VMEM((2, rows + 4, 2, full), jnp.float32),
             pltpu.VMEM((chunks, pad, tap_lanes), jnp.bfloat16),
+            pltpu.VMEM((rows, tap_lanes), jnp.float32),
+            pltpu.VMEM((2, 16, chans), jnp.float32),
+            pltpu.VMEM(weight_in.shape, jnp.bfloat16),
+            pltpu.VMEM(weight_out.shape, jnp.bfloat16),
+            sem((2,)),
             sem((14,)), sem((14,)),
             sem((chunks, n)), sem((chunks, n)), sem((chunks, n)), sem((chunks, n)),
         ],
@@ -324,7 +341,7 @@
             collective_id=0, has_side_effects=True, vmem_limit_bytes=60 * 2**20
         ),
     )(
-        inputs, spread, tb, lr, k_one, kernel_two, kept, norm_gain.reshape(1, chans),
+        inputs, metric, kernel_one, kernel_two, widths, zonal_gains, norm_gain.reshape(1, chans),
         weight_in, weight_out,
     )
     return out[:, :cols]

time: 71.3 us -> 63.9 us (0.90)
  other arithmetic: 4.47 us -> 0 us
  local copies, waits for them, and re-layouts: 9.41 us -> 6.69 us
    unnamed x5 -> x1, local copies, waits for them, and re-layouts: 0.82 us -> 3.34 us
    another operation x3 -> x0, other arithmetic: 2.42 us -> none  [the longest x1 1.4 us: local(): k_one = jnp.stack([kernel_one, flipped])]
    broadcast_in_dim x4 -> x0, local copies, waits for them, and re-layouts: 2.14 us -> none  [the longest x1 1.87 us: local(): spread = jnp.broadcast_to(metric[:, :, None], (rows, cols, LANES))]
    slice x3 -> x0, local copies, waits for them, and re-layouts: 1.7 us -> none  [the longest x1 0.86 us: local(): metric[:, :2]]
    concatenate x2 -> x0, other arithmetic: 0.99 us -> none  [the longest x1 0.98 us: packed(): return jnp.concatenate([first, spread], axis=2)]
    select_n x1 -> x0, other arithmetic: 0.79 us -> none  [local(): jnp.where(offsets[None, :] <= widths[:, None], zonal_gains.astype(jnp.flo...]
    reshape x1 -> x0, local copies, waits for them, and re-layouts: 0.77 us -> none  [local(): flipped = kernel_one.reshape(3, 3, chans)[::-1].reshape(9, chans)]
where the time goes in v2:
time: 63.9 us; the launch traced here: 63.7 us
  Pallas kernels  57 us (89%)
  local copies, waits for them, and re-layouts  6.69 us (10%)
    pallas_call x1, Pallas kernels, local(): pl.pallas_call(functools.partial(body, lats, n, rows, cols, chans, pad, r...  57 us
    slice x1, local copies, waits for them, and re-layouts, local(): return out[:, :cols]  3.35 us
    unnamed x1, local copies, waits for them, and re-layouts  3.34 us

profile of v2, /device:TPU:0, one launch (start us, length us, event | category | flops | bytes accessed | tf_op | source)
XLA Modules:
  0.0 63.7 jit_solution(15928362832220745345)
XLA Ops:
  0.0 3.3 %copy.10.x_ref = bf16[32,45,512]{2,1,0:T(8,128)(2,1)} copy(bf16[32,45,512]{2,0,1:T(8,128)(2,1)} %param.9) | data formatting | bytes 2949120 | tf_op args[0]
  3.3 57.0 %shard_map.91 = bf16[32,48,512]{2,1,0:T(8,128)(2,1)} custom-call(bf16[32,45,512]{2,1,0:T(8,128)(2,1)} %copy.10.x_ref, f32[32,45]{1,0:T(8,128)} %metric_ref.1, f32[9,512]{1,0:T(8,128)} %k1_ref.1, f32[9,512]{1,0:T(8,128)} %k2_ref.1, s32[32]{0:T(128)} %widths_ref.1, bf16[32,181]{1,0:T(8,128)(2,1)} %gains_ref.1, f32[1,512]{1,0:T(1,128)} %bitcast.3, ...), custom_call_target="tpu_custom_call" | custom-call | tf_op jit(solution)/shard_map/pallas_call | solution.py:313
  60.4 3.3 %copy.11 = bf16[32,45,512]{2,0,1:T(8,128)(2,1)} copy(bf16[32,45,512]{2,1,0:T(8,128)(2,1)} %bitcast.2) | data formatting | bytes 2949120 | tf_op jit(solution)/shard_map/slice | solution.py:347

commit v3 on v2

--- a/solution.py
+++ b/solution.py
@@ -24,7 +24,8 @@
     lats, n, rows, cols, chans, pad, reach,
     x_ref, metric_ref, k1_ref, k2_ref, widths_ref, gains_ref, gain_ref, win_hbm, wout_hbm,
     out_ref,
-    ext, sec, held, acc, mix, circ, zsend, zrecv, lr_ref, side, taps, lines, taps_one, win_ref, wout_ref,
+    ext, sec, held, acc, mix, circ, zsend, zrecv, flatx, edge, edge_in, strip, strip_in, rim, rim_in,
+    taps, lines, taps_one, win_ref, wout_ref,
     w_sem,
     hs_sem, hr_sem, fs_sem, fr_sem, rs_sem, rr_sem,
 ):
@@ -76,6 +77,10 @@
         jnp.int32, (pad, cols), 1
     )
 
+    for c in range(chans // LANES):
+        lanes = slice(c * LANES, (c + 1) * LANES)
+        flatx[c] = x_ref[:, :, lanes].astype(jnp.float32).reshape(cols * rows, LANES)
+
     def place(i, carry):
         line = jnp.broadcast_to(metric_ref[pl.ds(i, 1), :], (pad, cols))
         column = jnp.sum(jnp.where(diagonal, line, 0.0), axis=1, keepdims=True)
@@ -83,19 +88,21 @@
         ext[i + 2, pad:wide, :] = jnp.zeros((wide - pad, full), jnp.float32)
         held[i, pad - 8:pad, :] = jnp.zeros((8, chans), jnp.float32)
         ext[i + 2, LEAD:wide, chans:] = weight
-        lr_ref[0, i, :, chans:] = weight[0:2]
-        lr_ref[1, i, :, chans:] = weight[cols - 2:cols]
+        rim[0, i] = weight[0:1]
+        rim[1, i] = weight[cols - 1:cols]
         for c in range(chans // LANES):
             lanes = slice(c * LANES, (c + 1) * LANES)
-            cells = x_ref[i, :, lanes].astype(jnp.float32)
+            cells = flatx[c, pl.ds(i, cols, stride=rows), :]
             held[i, 0:cols, lanes] = cells
             first = (cells * weight[0:cols]).astype(jnp.bfloat16).astype(jnp.float32)
             ext[i + 2, LEAD:LEAD + cols, lanes] = first
-            lr_ref[0, i, :, lanes] = first[0:2]
-            lr_ref[1, i, :, lanes] = first[cols - 2:cols]
+            strip[0, i, :, lanes] = first[0:2].astype(jnp.bfloat16)
+            strip[1, i, :, lanes] = first[cols - 2:cols].astype(jnp.bfloat16)
         return carry
 
     lax.fori_loop(0, rows, place, 0)
+    for slot, row in enumerate((2, 3, rows, rows + 1)):
+        edge[slot] = ext[row, LEAD:wide, 0:chans].astype(jnp.bfloat16)
     pl.semaphore_wait(barrier, len(greeted))
 
     halo = []
@@ -111,8 +118,9 @@
     def slot_row(slot):
         return jnp.where(slot < 2, slot, rows + slot)
 
-    send_halo(lr_ref.at[0], side.at[1, pl.ds(2, rows)], 5, (lat, left))
-    send_halo(lr_ref.at[1], side.at[0, pl.ds(2, rows)], 4, (lat, right))
+    for s, device in ((0, left), (1, right)):
+        send_halo(strip.at[s], strip_in.at[1 - s, pl.ds(2, rows)], 4 + s, (lat, device))
+        send_halo(rim.at[s], rim_in.at[1 - s, pl.ds(2, rows)], 6 + s, (lat, device))
     for i in range(2):
         up_slot = jnp.where(at_top, 1 - i, 2 + i)
         down_slot = jnp.where(at_bottom, 3 - i, i)
@@ -120,18 +128,28 @@
             (up_slot, i, up_lat, up_lon),
             (down_slot, rows - 2 + i, down_lat, down_lon),
         ):
+            source = i if src_row < 2 else 2 + i
             dst_row = slot_row(slot)
-            send_halo(
-                ext.at[src_row + 2, pl.ds(LEAD, pad)], ext.at[dst_row, pl.ds(LEAD, pad)], slot, (device_lat, device_lon)
-            )
-            send_halo(
-                lr_ref.at[0, src_row], side.at[1, dst_row], 10 + slot,
-                (device_lat, before(device_lon)),
-            )
-            send_halo(
-                lr_ref.at[1, src_row], side.at[0, dst_row], 6 + slot,
-                (device_lat, after(device_lon)),
-            )
+            target = (device_lat, device_lon)
+            send_halo(edge.at[source], edge_in.at[slot], slot, target)
+            corners = ((0, before(device_lon)), (1, after(device_lon)))
+            for s, corner_lon in corners:
+                send_halo(
+                    strip.at[s, src_row], strip_in.at[1 - s, dst_row], 8 + 4 * s + slot,
+                    (device_lat, corner_lon),
+                )
+            if src_row in (0, rows - 1):
+                near = jnp.where(slot < 2, 0, 1)
+                send_halo(
+                    ext.at[src_row + 2, pl.ds(LEAD, pad), pl.ds(chans, LANES)],
+                    ext.at[dst_row, pl.ds(LEAD, pad), pl.ds(chans, LANES)],
+                    16 + near, target,
+                )
+                for s, corner_lon in corners:
+                    send_halo(
+                        rim.at[s, src_row], rim_in.at[1 - s, dst_row], 18 + 2 * s + near,
+                        (device_lat, corner_lon),
+                    )
 
     tap_lanes = taps.shape[2]
     lane_ids = lax.broadcasted_iota(jnp.int32, (pad, tap_lanes), 1)
@@ -161,21 +179,38 @@
         ).wait_recv()
 
     for s in range(2):
-        recv_halo(lr_ref.at[s], side.at[s, pl.ds(2, rows)], 4 + s)
+        recv_halo(strip.at[s], strip_in.at[1 - s, pl.ds(2, rows)], 4 + s)
+        recv_halo(rim.at[s], rim_in.at[1 - s, pl.ds(2, rows)], 6 + s)
+        row = (1, rows + 2)[s]
+        recv_halo(
+            ext.at[2, pl.ds(LEAD, pad), pl.ds(chans, LANES)],
+            ext.at[row, pl.ds(LEAD, pad), pl.ds(chans, LANES)], 16 + s,
+        )
+        for near in range(2):
+            recv_halo(rim.at[s, 0], rim_in.at[1 - s, (1, rows + 2)[near]], 18 + 2 * s + near)
     for slot in range(4):
         row = slot if slot < 2 else rows + slot
-        recv_halo(ext.at[2, pl.ds(LEAD, pad)], ext.at[row, pl.ds(LEAD, pad)], slot)
+        recv_halo(edge.at[0], edge_in.at[slot], slot)
         for s in range(2):
-            recv_halo(lr_ref.at[0, 0], side.at[s, row], 6 + 4 * s + slot)
-
+            recv_halo(strip.at[s, 0], strip_in.at[1 - s, row], 8 + 4 * s + slot)
     for copy in halo:
         copy.wait_send()
 
+    for slot in range(4):
+        row = slot if slot < 2 else rows + slot
+        ext[row, LEAD:wide, 0:chans] = edge_in[slot].astype(jnp.float32)
+
     def join(e, carry):
-        ext[e, LEAD - 2:LEAD, :] = side[0, e]
-        ext[e, LEAD + cols:LEAD + cols + 2, :] = side[1, e]
-        return carry
-
+        for s, at in ((0, LEAD - 2), (1, LEAD + cols)):
+            ext[e, at:at + 2, 0:chans] = strip_in[s, e].astype(jnp.float32)
+        return carry
+
+    def join_rim(e, carry):
+        ext[e, LEAD - 1:LEAD, chans:] = rim_in[0, e]
+        ext[e, LEAD + cols:LEAD + cols + 1, chans:] = rim_in[1, e]
+        return carry
+
+    lax.fori_loop(1, rows + 3, join_rim, 0)
     lax.fori_loop(0, rows + 4, join, 0)
 
     def stencil(src, row, kernel, lanes):
@@ -326,22 +361,27 @@
             pltpu.VMEM((chunks, n + 2 * reach, pad, chans), jnp.bfloat16),
             pltpu.VMEM((rows, pad, chans), jnp.bfloat16),
             pltpu.VMEM((rows, pad, chans), jnp.bfloat16),
-            pltpu.VMEM((2, rows, 2, full), jnp.float32),
-            pltpu.VMEM((2, rows + 4, 2, full), jnp.float32),
+            pltpu.VMEM((chans // LANES, cols * rows, LANES), jnp.float32),
+            pltpu.VMEM((4, pad, chans), jnp.bfloat16),
+            pltpu.VMEM((4, pad, chans), jnp.bfloat16),
+            pltpu.VMEM((2, rows, 2, chans), jnp.bfloat16),
+            pltpu.VMEM((2, rows + 4, 2, chans), jnp.bfloat16),
+            pltpu.VMEM((2, rows, 1, LANES), jnp.float32),
+            pltpu.VMEM((2, rows + 4, 1, LANES), jnp.float32),
             pltpu.VMEM((chunks, pad, tap_lanes), jnp.bfloat16),
             pltpu.VMEM((rows, tap_lanes), jnp.float32),
             pltpu.VMEM((2, 16, chans), jnp.float32),
             pltpu.VMEM(weight_in.shape, jnp.bfloat16),
             pltpu.VMEM(weight_out.shape, jnp.bfloat16),
             sem((2,)),
-            sem((14,)), sem((14,)),
+            sem((22,)), sem((22,)),
             sem((chunks, n)), sem((chunks, n)), sem((chunks, n)), sem((chunks, n)),
         ],
         compiler_params=pltpu.CompilerParams(
             collective_id=0, has_side_effects=True, vmem_limit_bytes=60 * 2**20
         ),
     )(
-        inputs, metric, kernel_one, kernel_two, widths, zonal_gains, norm_gain.reshape(1, chans),
+        inputs.transpose(1, 0, 2), metric, kernel_one, kernel_two, widths, zonal_gains, norm_gain.reshape(1, chans),
         weight_in, weight_out,
     )
     return out[:, :cols]

time: 63.9 us -> 58 us (0.908)
  local copies, waits for them, and re-layouts: 6.69 us -> 3.35 us
  Pallas kernels: 57 us -> 54.5 us
    unnamed x1 -> x0, local copies, waits for them, and re-layouts: 3.34 us -> none
    pallas_call x1, Pallas kernels: 57 us -> 54.5 us  [local(): pl.pallas_call(functools.partial(body, lats, n, rows, cols, chans, pad, r...]
where the time goes in v3:
time: 58 us; the launch traced here: 57.9 us
  Pallas kernels  54.5 us (94%)
  local copies, waits for them, and re-layouts  3.35 us (6%)
    pallas_call x1, Pallas kernels, local(): pl.pallas_call(functools.partial(body, lats, n, rows, cols, chans, pad, r...  54.5 us
    slice x1, local copies, waits for them, and re-layouts, local(): return out[:, :cols]  3.35 us

profile of v3, /device:TPU:0, one launch (start us, length us, event | category | flops | bytes accessed | tf_op | source)
XLA Modules:
  0.0 57.9 jit_solution(13356090287612997143)
XLA Ops:
  0.0 54.5 %shard_map.91 = bf16[32,48,512]{2,1,0:T(8,128)(2,1)} custom-call(bf16[45,32,512]{2,1,0:T(8,128)(2,1)} %bitcast.4, f32[32,45]{1,0:T(8,128)} %metric_ref.1, f32[9,512]{1,0:T(8,128)} %k1_ref.1, f32[9,512]{1,0:T(8,128)} %k2_ref.1, s32[32]{0:T(128)} %widths_ref.1, bf16[32,181]{1,0:T(8,128)(2,1)} %gains_ref.1, f32[1,512]{1,0:T(1,128)} %bitcast.5, ...), custom_call_target="tpu_custom_call" | custom-call | tf_op jit(solution)/shard_map/pallas_call | solution.py:348
  54.5 3.3 %copy.10 = bf16[32,45,512]{2,0,1:T(8,128)(2,1)} copy(bf16[32,45,512]{2,1,0:T(8,128)(2,1)} %bitcast.3) | data formatting | bytes 2949120 | tf_op jit(solution)/shard_map/slice | solution.py:387

commit v4 on v3

--- a/solution.py
+++ b/solution.py
@@ -310,6 +310,7 @@
             back.append(copy)
         zrecv[k * n + me] = zsend[k * n + me]
 
+    done = 0
     for k in range(chunks):
         for o in range(1, n):
             source = lax.rem(me + n - o, n)
@@ -320,10 +321,20 @@
             ).wait_recv()
 
         def finish(i, carry):
-            out_ref[i] = (acc[i] + zrecv[i].astype(jnp.float32)).astype(jnp.bfloat16)
+            for c in range(chans // LANES):
+                lanes = slice(c * LANES, (c + 1) * LANES)
+                cells = acc[i, :, lanes] + zrecv[i, :, lanes].astype(jnp.float32)
+                flatx[c, pl.ds(i, cols, stride=rows), :] = cells[0:cols]
             return carry
 
         lax.fori_loop(k * n, (k + 1) * n, finish, 0)
+        low = done
+        done = (k + 1) * n // 16 * 16
+        if done > low:
+            for c in range(chans // LANES):
+                lanes = slice(c * LANES, (c + 1) * LANES)
+                block = flatx[c].reshape(cols, rows, LANES)[:, low:done]
+                out_ref[:, low:done, lanes] = block.astype(jnp.bfloat16)
 
     for copy in forward + back:
         copy.wait_send()
@@ -347,7 +358,7 @@
     sem = pltpu.SemaphoreType.DMA
     out = pl.pallas_call(
         functools.partial(body, lats, n, rows, cols, chans, pad, reach),
-        out_shape=jax.ShapeDtypeStruct((rows, pad, chans), jnp.bfloat16),
+        out_shape=jax.ShapeDtypeStruct((cols, rows, chans), jnp.bfloat16),
         in_specs=[vmem] * 4
         + [pl.BlockSpec(memory_space=pltpu.SMEM), vmem, vmem]
         + [pl.BlockSpec(memory_space=pl.ANY)] * 2,
@@ -384,7 +395,7 @@
         inputs.transpose(1, 0, 2), metric, kernel_one, kernel_two, widths, zonal_gains, norm_gain.reshape(1, chans),
         weight_in, weight_out,
     )
-    return out[:, :cols]
+    return out.transpose(1, 0, 2)
 
 
 def solution(mesh):

time: 58 us -> 58.1 us (level)
  Pallas kernels: 54.5 us -> 55.3 us
  local copies, waits for them, and re-layouts: 3.35 us -> 2.65 us
    slice x1 -> x0, local copies, waits for them, and re-layouts: 3.35 us -> none  [local(): return out[:, :cols]]
    unnamed x0 -> x1, local copies, waits for them, and re-layouts: none -> 2.65 us
    pallas_call x1, Pallas kernels: 54.5 us -> 55.3 us  [local(): pl.pallas_call(functools.partial(body, lats, n, rows, cols, chans, pad, r...]
where the time goes in v4:
time: 58.1 us; the launch traced here: 58 us
  Pallas kernels  55.3 us (95%)
  local copies, waits for them, and re-layouts  2.65 us (5%)
    pallas_call x1, Pallas kernels, local(): pl.pallas_call(functools.partial(body, lats, n, rows, cols, chans, pad, r...  55.3 us
    unnamed x1, local copies, waits for them, and re-layouts  2.65 us

profile of v4, /device:TPU:0, one launch (start us, length us, event | category | flops | bytes accessed | tf_op | source)
XLA Modules:
  0.0 58.0 jit_solution(15162658775646256637)
XLA Ops:
  0.0 55.3 %shard_map.91 = bf16[45,32,512]{2,1,0:T(8,128)(2,1)} custom-call(bf16[45,32,512]{2,1,0:T(8,128)(2,1)} %bitcast.4, f32[32,45]{1,0:T(8,128)} %metric_ref.1, f32[9,512]{1,0:T(8,128)} %k1_ref.1, f32[9,512]{1,0:T(8,128)} %k2_ref.1, s32[32]{0:T(128)} %widths_ref.1, bf16[32,181]{1,0:T(8,128)(2,1)} %gains_ref.1, f32[1,512]{1,0:T(1,128)} %bitcast.5, ...), custom_call_target="tpu_custom_call" | custom-call | tf_op jit(solution)/shard_map/pallas_call | solution.py:359
  55.3 2.7 %copy.11 = bf16[32,45,512]{2,0,1:T(8,128)(2,1)} copy(bf16[32,45,512]{2,0,1:T(8,128)(2,1)} %bitcast.3) | data formatting | bytes 2949120

commit v5 on v3

--- a/solution.py
+++ b/solution.py
@@ -22,10 +22,10 @@
 
 def body(
     lats, n, rows, cols, chans, pad, reach,
-    x_ref, metric_ref, k1_ref, k2_ref, widths_ref, gains_ref, gain_ref, win_hbm, wout_hbm,
+    x_hbm, metric_ref, k1_ref, k2_ref, widths_ref, gains_ref, gain_ref, win_hbm, wout_hbm,
     out_ref,
     ext, sec, held, acc, mix, circ, zsend, zrecv, flatx, edge, edge_in, strip, strip_in, rim, rim_in,
-    taps, lines, taps_one, win_ref, wout_ref,
+    taps, lines, taps_one, win_ref, wout_ref, x_ref,
     w_sem,
     hs_sem, hr_sem, fs_sem, fr_sem, rs_sem, rr_sem,
 ):
@@ -53,6 +53,7 @@
         return lax.rem(lon + 1, n)
 
     loads = [
+        pltpu.make_async_copy(x_hbm, x_ref, w_sem.at[2]),
         pltpu.make_async_copy(win_hbm, win_ref, w_sem.at[0]),
         pltpu.make_async_copy(wout_hbm, wout_ref, w_sem.at[1]),
     ]
@@ -77,6 +78,7 @@
         jnp.int32, (pad, cols), 1
     )
 
+    loads[0].wait()
     for c in range(chans // LANES):
         lanes = slice(c * LANES, (c + 1) * LANES)
         flatx[c] = x_ref[:, :, lanes].astype(jnp.float32).reshape(cols * rows, LANES)
@@ -259,7 +261,7 @@
             forward.append(copy)
         circ[k, me + reach] = mix[k * n + me]
 
-    for load in loads:
+    for load in loads[1:]:
         load.wait()
 
     group = 8
@@ -348,7 +350,7 @@
     out = pl.pallas_call(
         functools.partial(body, lats, n, rows, cols, chans, pad, reach),
         out_shape=jax.ShapeDtypeStruct((rows, pad, chans), jnp.bfloat16),
-        in_specs=[vmem] * 4
+        in_specs=[pl.BlockSpec(memory_space=pl.ANY)] + [vmem] * 3
         + [pl.BlockSpec(memory_space=pltpu.SMEM), vmem, vmem]
         + [pl.BlockSpec(memory_space=pl.ANY)] * 2,
         out_specs=vmem,
@@ -373,7 +375,8 @@
             pltpu.VMEM((2, 16, chans), jnp.float32),
             pltpu.VMEM(weight_in.shape, jnp.bfloat16),
             pltpu.VMEM(weight_out.shape, jnp.bfloat16),
-            sem((2,)),
+            pltpu.VMEM((cols, rows, chans), jnp.bfloat16),
+            sem((3,)),
             sem((22,)), sem((22,)),
             sem((chunks, n)), sem((chunks, n)), sem((chunks, n)), sem((chunks, n)),
         ],

time: 58 us -> 58.5 us (level)
  no operation moved by 1% of the time
where the time goes in v5:
time: 58.5 us; the launch traced here: 58.3 us
  Pallas kernels  55 us (94%)
  local copies, waits for them, and re-layouts  3.35 us (6%)
    pallas_call x1, Pallas kernels, local(): pl.pallas_call(functools.partial(body, lats, n, rows, cols, chans, pad, r...  55 us
    slice x1, local copies, waits for them, and re-layouts, local(): return out[:, :cols]  3.35 us

profile of v5, /device:TPU:0, one launch (start us, length us, event | category | flops | bytes accessed | tf_op | source)
XLA Modules:
  0.0 58.3 jit_solution(8053935339116741865)
XLA Ops:
  0.0 55.0 %shard_map.91 = bf16[32,48,512]{2,1,0:T(8,128)(2,1)} custom-call(bf16[45,32,512]{2,1,0:T(8,128)(2,1)} %bitcast.4, f32[32,45]{1,0:T(8,128)} %metric_ref.1, f32[9,512]{1,0:T(8,128)} %k1_ref.1, f32[9,512]{1,0:T(8,128)} %k2_ref.1, s32[32]{0:T(128)} %widths_ref.1, bf16[32,181]{1,0:T(8,128)(2,1)} %gains_ref.1, f32[1,512]{1,0:T(1,128)} %bitcast.5, ...), custom_call_target="tpu_custom_call" | custom-call | tf_op jit(solution)/shard_map/pallas_call | solution.py:350
  55.0 3.3 %copy.10 = bf16[32,45,512]{2,0,1:T(8,128)(2,1)} copy(bf16[32,45,512]{2,1,0:T(8,128)(2,1)} %bitcast.3) | data formatting | bytes 2949120 | tf_op jit(solution)/shard_map/slice | solution.py:390
